TPU v7x, 256 devices: a whole 4x4x8 slice. The times are simulated.
256 devices in a mesh: half: 2 (over core), row: 8 (over z_hi, x), col: 16 (over y, z_lo).
Axes of the slice: x: 4, y: 4, z: 8 (z_hi: 2, z_lo: 4; z = z_hi * 4 + z_lo), core: 2. Of those that a mesh axis runs over, the one named last changes fastest.
Arguments:
- parent_front: float32 [16384, 16384], P(('half', 'row'), 'col'), may hold values from -6 to 6
- child_blocks: float32 [2, 8192, 8192], P('half', 'row', 'col'), may hold values from -6 to 6
- row_maps: int32 [2, 8192], replicated, may hold values from 0 to 16383, as said below
- inverse_blocks: float32 [4, 128, 128], replicated, may hold values from -0.12 to 0.12
Outputs:
- updated_front: float32 [16384, 16384], P(('half', 'row'), 'col')
- panel_factor: bfloat16 [16384, 512], P(('half', 'row'))
Inputs may be any that keep to these rules, and one draw needn't show every extreme that they name: `row_maps`: each row lists 8192 distinct parent rows. In every aligned block of 512 entries of a row, at most 64 entries fall in one aligned block of 1024 parent rows, and that bound is reached in every such block; in every aligned block of 1024 entries, at most 128 fall in one aligned block of 1024 parent rows, and that bound is reached in every such block.
All inputs are finite; a program needn't handle non-finite values.
Results may differ from a plain program's by a relative error of at most 0.001.
Values sent between devices are 32-bit elements; how exact they have to be, the bound alone decides.
A program may use at most 128 MiB of HBM per device.

v0:
```python
import jax
import jax.numpy as jnp
from jax import lax
from jax.sharding import PartitionSpec as P


def from_root(block, axis, holder):
    block = jnp.where(lax.axis_index(axis) == holder, block, jnp.zeros_like(block))
    return lax.psum(block, axis)


def highest_outer(left, right):
    return lax.dot_general(
        left,
        right,
        (((1,), (1,)), ((), ())),
        precision=lax.Precision.HIGHEST,
        preferred_element_type=jnp.float32,
    )


def ranks(targets, count):
    onehot = (targets[..., None] == jnp.arange(count, dtype=jnp.int32)).astype(jnp.int32)
    before = jnp.cumsum(onehot, axis=-2) - onehot
    return jnp.sum(before * onehot, axis=-1)


def row_tables(row_maps, row_loc, groups, cap_rows, my_group):
    parent_rows = row_maps.reshape(groups, -1)
    targets = parent_rows // row_loc
    slots = ranks(targets, groups)
    sources = jnp.arange(groups, dtype=jnp.int32)[:, None]
    where_at = jnp.where(targets == my_group, sources * cap_rows + slots, groups * cap_rows)
    table = (
        jnp.full((groups * cap_rows,), row_loc, jnp.int32)
        .at[where_at.reshape(-1)]
        .set((parent_rows % row_loc).reshape(-1), mode="drop")
    )
    send_at = targets[my_group] * cap_rows + slots[my_group]
    return (send_at, table)


def col_tables(row_maps, col_loc, n_col, cap_cols, my_col):
    parent_cols = row_maps.reshape(2, n_col, -1)
    targets = parent_cols // col_loc
    slots = ranks(targets, n_col)
    sources = jnp.arange(n_col, dtype=jnp.int32)[None, :, None]
    where_at = jnp.where(targets == my_col, sources * cap_cols + slots, n_col * cap_cols)
    child_index = jnp.broadcast_to(jnp.arange(2, dtype=jnp.int32)[:, None, None], where_at.shape)
    table = (
        jnp.full((2, n_col * cap_cols), col_loc, jnp.int32)
        .at[child_index, where_at]
        .set(parent_cols % col_loc, mode="drop")
    )
    send_at = targets[:, my_col] * cap_cols + slots[:, my_col]
    return (send_at, table)


def row_pack(values, send_at, total):
    return jnp.zeros((total, values.shape[1]), values.dtype).at[send_at].set(values)


def col_pack(values, send_at, total):
    return jnp.zeros((values.shape[0], total), values.dtype).at[:, send_at].set(values)


def local(parent_front, child_blocks, row_maps, inverse_blocks):
    row_loc, col_loc = parent_front.shape
    child_rows, child_cols = (child_blocks.shape[1], child_blocks.shape[2])
    n_row = lax.axis_size("row")
    n_col = lax.axis_size("col")
    groups = lax.axis_size("half") * n_row
    my_child = lax.axis_index("half")
    my_group = my_child * n_row + lax.axis_index("row")
    my_col = lax.axis_index("col")
    cap_cols = 2 * child_cols // n_col
    cap_rows = n_col // n_row * (child_cols // groups + child_cols // n_col)
    slab_rows = n_row * cap_rows
    row_send, row_table = row_tables(row_maps, row_loc, groups, cap_rows, my_group)
    col_send, col_table = col_tables(row_maps, col_loc, n_col, cap_cols, my_col)
    mine = child_blocks[0]
    moved = row_pack(mine, row_send, groups * cap_rows)
    arrived = lax.all_to_all(
        moved, ("half", "row"), split_axis=0, concat_axis=0, tiled=True
    ).reshape(2, slab_rows, child_cols)
    outgoing = jnp.stack(
        [col_pack(arrived[child], col_send[child], n_col * cap_cols) for child in range(2)]
    )
    landed = lax.all_to_all(outgoing, "col", split_axis=2, concat_axis=2, tiled=True)
    row_dest = row_table.reshape(2, slab_rows)
    assembled = parent_front
    for child in range(2):
        spread = (
            jnp.zeros((slab_rows, col_loc), jnp.float32)
            .at[:, col_table[child]]
            .add(landed[child], mode="drop")
        )
        assembled = assembled.at[row_dest[child]].add(spread, mode="drop")
    width = inverse_blocks.shape[1]
    count = inverse_blocks.shape[0]
    span = n_col // groups
    root = my_col // span
    factors = []
    tops = []
    for block in range(count):
        current = assembled[:, block * width : (block + 1) * width]
        if block > 0:
            earlier = jnp.concatenate(factors, axis=1)
            above = jnp.concatenate(
                [
                    tops[prior][(block - prior - 1) * width : (block - prior) * width]
                    for prior in range(block)
                ],
                axis=1,
            )
            current = current - highest_outer(earlier, above)
        result = highest_outer(current, jnp.tril(inverse_blocks[block]))
        factors.append(result)
        if block + 1 < count:
            tops.append(from_root(result[(block + 1) * width : count * width], ("half", "row"), 0))
    local_factor = jnp.concatenate(factors, axis=1)
    factor_rows = from_root(local_factor, "col", 0)
    factor_cols = from_root(factor_rows, ("half", "row"), root)
    updated_front = assembled - highest_outer(factor_rows, factor_cols)
    return (updated_front, factor_rows.astype(jnp.bfloat16))


def solution(mesh):
    in_specs = (P(("half", "row"), "col"), P("half", "row", "col"), P(), P())
    out_specs = (P(("half", "row"), "col"), P(("half", "row"), None))
    return jax.shard_map(local, mesh=mesh, in_specs=in_specs, out_specs=out_specs, check_vma=False)
```

profile of v0, /device:TPU:1, one launch (start us, length us, event | category | flops | bytes accessed | tf_op | source)
XLA Modules:
  0.0 1522.6 jit_solution(5224957147716496916)
XLA Ops:
  7.2 5.0 copy.95
  12.3 1.1 fusion.34
  13.4 123.6 %reduce-window.14 = s32[16,16,8,128]{3,2,1,0:T(8,128)S(1)} reduce-window(s32[16,16,8,128]{3,2,1,0:T(8,128)} %fusion.34, s32[]{:T(128)} %constant.102.clone.1), window={size=1x1x1x128 pad=0_0x0_0x0_0x127_0}, to_apply=%region_0.1 | reduce-window | flops 33292288 | bytes 2097156 | tf_op jit(solution)/shard_map/reduce-window
  137.0 1.3 slice.136
  138.3 2.0 copy.27
  140.5 1.3 broadcast_add_fusion
  141.8 1.4 reduce_window_sum.31
  143.6 7.1 scatter_custom_fusion.1
  150.7 12.4 all-to-all-start
  163.5 36.3 %reduce-window.16 = s32[2,16,16,4,128]{4,2,3,1,0:T(8,128)S(1)} reduce-window(s32[2,16,16,4,128]{4,2,3,1,0:T(8,128)S(1)} %fusion.35, s32[]{:T(128)} %constant.102.clone.1), window={size=1x1x1x1x128 pad=0_0x0_0x0_0x0_0x127_0}, to_apply=%region_4.5 | reduce-window | flops 33292288 | bytes 2097156 | tf_op jit(solution)/shard_map/reduce-window.2
  200.1 0.8 copy.29
  201.9 59.7 %all-to-all-done = f32[16,128,512]{2,1,0:T(8,128)} async-done(((f32[16,128,512]{2,1,0:T(8,128)}), f32[16,128,512]{2,1,0:T(8,128)}, u32[]{:S(2)}, u32[]{:S(2)}) %all-to-all-start) | async-done | bytes 4194336 | tf_op jit(solution)/shard_map/all_to_all | solution.py:83
  261.6 4.2 fusion.82
  265.7 1.8 copy.42
  267.6 1.9 copy.43
  269.5 5.7 scatter_custom_fusion.2
  275.2 4.6 scatter_custom_fusion.3
  279.8 4.3 pad_maximum_fusion
  284.1 13.0 copy.34
  297.1 5.8 all-to-all-start.1
  303.7 60.3 %scatter_custom_fusion.8 = s32[2048]{0:T(1024)S(1)} fusion(s32[16384]{0:T(1024)S(1)} %bitcast.176, s32[16384]{0:T(1024)S(1)} %bitcast.177, s32[]{:T(128)} %constant.100.clone.1), kind=kCustom, calls=%fused_computation.152 | custom fusion | bytes 8196
  364.5 60.5 %scatter_custom_fusion = s32[2048]{0:T(1024)S(1)} fusion(s32[16384]{0:T(1024)S(1)} %bitcast.175, s32[16384]{0:T(1024)S(1)} %add_select_fusion.4, s32[]{:T(128)} %constant.100.clone.1), kind=kCustom, calls=%fused_computation.154 | custom fusion | bytes 8196 | tf_op jit(solution)/shard_map/scatter | solution.py:37
  425.0 63.9 %all-to-all-done.1 = f32[2,1024,1024]{1,0,2:T(2,128)} async-done(((f32[2,1024,1024]{1,0,2:T(2,128)}), f32[2,1024,1024]{1,0,2:T(2,128)}, u32[]{:S(2)}, u32[]{:S(2)}) %all-to-all-start.1) | async-done | bytes 8388640 | tf_op jit(solution)/shard_map/all_to_all | solution.py:89
  489.0 11.6 fusion.81
  500.5 13.6 scatter_custom_fusion.4
  514.1 5.3 copy.35
  519.5 14.0 scatter_custom_fusion.6
  533.4 5.3 copy.36
  538.8 14.4 scatter_fusion
  553.2 14.4 scatter_fusion.1
  567.7 1.7 fusion.36
  569.4 0.7 slice_select_fusion
  570.3 174.1 %all-reduce.6.cloned.1.call-done = f32[384,128]{0,1:T(8,128)} async-done(((f32[384,128]{0,1:T(8,128)}), f32[384,128]{0,1:T(8,128)}) %all-reduce.6.cloned.1.call-update) | async-done | bytes 196624 | tf_op jit(solution)/shard_map/psum | solution.py:9
  744.4 2.1 convolution_subtract_fusion.2
  747.1 0.7 slice_select_fusion.1
  747.9 0.9 fusion.85
  748.8 184.5 %all-reduce.8.cloned.1.call-done = f32[256,128]{0,1:T(8,128)} async-done(((f32[256,128]{0,1:T(8,128)}), f32[256,128]{0,1:T(8,128)}) %all-reduce.8.cloned.1.call-update) | async-done | bytes 131088 | tf_op jit(solution)/shard_map/psum | solution.py:9
  933.3 0.9 fusion.86
  934.2 2.9 convolution_subtract_fusion.1
  937.6 0.6 slice_select_fusion.2
  938.6 177.9 %all-reduce.10.cloned.1.call-done = f32[128,128]{0,1:T(8,128)} async-done(((f32[128,128]{0,1:T(8,128)}), f32[128,128]{0,1:T(8,128)}) %all-reduce.10.cloned.1.call-update) | async-done | bytes 65552 | tf_op jit(solution)/shard_map/psum | solution.py:9
  1116.5 3.8 fusion.23
  1121.0 1.6 maximum_select_fusion
  1122.6 166.6 %all-reduce.12.cloned.1.call-done = f32[1024,512]{0,1:T(8,128)} async-done(((f32[1024,512]{0,1:T(8,128)}), f32[1024,512]{0,1:T(8,128)}) %all-reduce.12.cloned.1.call-update) | async-done | bytes 2097168 | tf_op jit(solution)/shard_map/psum | solution.py:9
  1289.2 4.1 fusion.83
  1293.3 1.3 copy.41
  1294.6 210.5 %all-reduce.14.cloned.1.call-done = f32[1024,512]{0,1:T(8,128)} async-done(((f32[1024,512]{0,1:T(8,128)}), f32[1024,512]{0,1:T(8,128)}) %all-reduce.14.cloned.1.call-update) | async-done | bytes 2097168 | tf_op jit(solution)/shard_map/psum | solution.py:9
  1505.1 10.8 convolution_subtract_fusion
  (69 shorter events, 5.9 us)
Async XLA Ops:
  7.2 136.5 %copy-start = (f32[1,1024,512]{2,1,0:T(8,128)S(1)}, f32[1,1024,512]{2,1,0:T(8,128)}, u32[]{:S(2)}) copy-start(f32[1,1024,512]{2,1,0:T(8,128)} %param.5) | copy-start | bytes 6291460
  7.2 5.0 copy-start.2
  150.7 110.8 %all-to-all-start = ((f32[16,128,512]{2,1,0:T(8,128)}), f32[16,128,512]{2,1,0:T(8,128)}, u32[]{:S(2)}, u32[]{:S(2)}) async-start(f32[16,128,512]{2,1,0:T(8,128)} %bitcast.160), calls=%async_computation | async-start | bytes 8388608 | tf_op jit(solution)/shard_map/all_to_all | solution.py:83
  297.1 6.0 copy-start.5
  297.1 6.1 copy-start.4
  297.1 6.5 copy-start.3
  297.1 191.9 %all-to-all-start.1 = ((f32[2,1024,1024]{1,0,2:T(2,128)}), f32[2,1024,1024]{1,0,2:T(2,128)}, u32[]{:S(2)}, u32[]{:S(2)}) async-start(f32[2,1024,1024]{1,0,2:T(2,128)} %copy.34), calls=%async_computation.1 | async-start | bytes 16777216 | tf_op jit(solution)/shard_map/all_to_all | solution.py:89
  302.9 441.5 %all-reduce.6.cloned.1.call-start = ((), (), s32[]{:S(2)}) async-start(), calls=%async_computation.2 | async-start | bytes 393216 | tf_op jit(solution)/shard_map/psum | solution.py:9
  570.1 363.2 %all-reduce.8.cloned.1.call-start = ((), (), s32[]{:S(2)}) async-start(), calls=%async_computation.3 | async-start | bytes 262144 | tf_op jit(solution)/shard_map/psum | solution.py:9
  747.8 368.7 %all-reduce.10.cloned.1.call-start = ((), (), s32[]{:S(2)}) async-start(), calls=%async_computation.4 | async-start | bytes 131072 | tf_op jit(solution)/shard_map/psum | solution.py:9
  938.3 350.9 %all-reduce.12.cloned.1.call-start = ((), (), s32[]{:S(2)}) async-start(), calls=%async_computation.5 | async-start | bytes 4194304 | tf_op jit(solution)/shard_map/psum | solution.py:9
  1122.6 382.5 %all-reduce.14.cloned.1.call-start = ((), (), s32[]{:S(2)}) async-start(), calls=%async_computation.6 | async-start | bytes 4194304 | tf_op jit(solution)/shard_map/psum | solution.py:9
  1293.3 222.6 %copy-start.1 = (f32[1,1024,512]{2,1,0:T(8,128)S(1)}, f32[1,1024,512]{2,1,0:T(8,128)}, u32[]{:S(2)}) copy-start(f32[1,1024,512]{2,1,0:T(8,128)} %param.5) | copy-start | bytes 6291460
Sparse Core Ops, SparseCore 0:
  570.2 174.1 all-reduce.5
  748.0 185.2 all-reduce.7
  938.4 178.0 all-reduce.9
  1122.7 166.4 all-reduce.11
  1293.4 211.6 all-reduce.13
where the time goes:
time: 1540 us; the launch traced here: 1520 us
  waiting for transfers between devices  1040 us (68%)
  other arithmetic  233 us (15%)
  local copies, waits for them, and re-layouts  196 us (13%)
  matrix products  23.1 us (2%)
  starting transfers between devices  18.6 us (1%)
    psum x5, waiting for transfers between devices, from_root(): return lax.psum(block, axis)  913 us
    another operation x5, other arithmetic  161 us
    unnamed x24, local copies, waits for them, and re-layouts  67.2 us
    all_to_all x1, waiting for transfers between devices, local(): lax.all_to_all(outgoing, 'col', split_axis=2, concat_axis=2, tiled=True)  63.9 us
    scatter x1, local copies, waits for them, and re-layouts, row_tables(): table = jnp.full((groups * cap_rows,), row_loc, jnp.int32).at[where_at.re...  60.5 us
    all_to_all x1, waiting for transfers between devices, local(): lax.all_to_all(moved, ('half', 'row'), split_axis=0, concat_axis=0, tiled...  59.7 us
  transfers between devices with their start and end apart: 7, of which 7 were waited for; matrix products, arithmetic and copies ran while one was open for 11% of the time, Pallas kernels for 0%

commit v1 on v0

--- a/solution.py
+++ b/solution.py
@@ -86,7 +86,10 @@
     outgoing = jnp.stack(
         [col_pack(arrived[child], col_send[child], n_col * cap_cols) for child in range(2)]
     )
-    landed = lax.all_to_all(outgoing, "col", split_axis=2, concat_axis=2, tiled=True)
+    landed = jnp.concatenate(
+        lax.all_to_all(jnp.stack(jnp.split(outgoing, lax.axis_size("col"), axis=2)), "col", 0, 0),
+        axis=2,
+    )
     row_dest = row_table.reshape(2, slab_rows)
     assembled = parent_front
     for child in range(2):

time: 1540 us -> 1530 us (level)
    unnamed x24 -> x28, local copies, waits for them, and re-layouts: 67.2 us -> 68.9 us
where the time goes in v1:
time: 1530 us; the launch traced here: 1520 us
  waiting for transfers between devices  1040 us (68%)
  other arithmetic  241 us (16%)
  local copies, waits for them, and re-layouts  182 us (12%)
  matrix products  23.1 us (2%)
  starting transfers between devices  18.7 us (1%)
    psum x5, waiting for transfers between devices, from_root(): return lax.psum(block, axis)  914 us
    another operation x5, other arithmetic  161 us
    unnamed x28, local copies, waits for them, and re-layouts  68.9 us
    all_to_all x1, waiting for transfers between devices, local(): lax.all_to_all(jnp.stack(jnp.split(outgoing, lax.axis_size('col'), axis=2...  64.2 us
    scatter x1, local copies, waits for them, and re-layouts, row_tables(): table = jnp.full((groups * cap_rows,), row_loc, jnp.int32).at[where_at.re...  60.3 us
    all_to_all x1, waiting for transfers between devices, local(): lax.all_to_all(moved, ('half', 'row'), split_axis=0, concat_axis=0, tiled...  59.7 us
  transfers between devices with their start and end apart: 7, of which 7 were waited for; matrix products, arithmetic and copies ran while one was open for 11% of the time, Pallas kernels for 0%

profile of v1, /device:TPU:1, one launch (start us, length us, event | category | flops | bytes accessed | tf_op | source)
XLA Modules:
  0.0 1516.9 jit_solution(17354515607382744835)
XLA Ops:
  7.2 5.0 copy.85
  12.3 1.1 fusion.30
  13.4 123.6 %reduce-window.14 = s32[16,16,8,128]{3,2,1,0:T(8,128)S(1)} reduce-window(s32[16,16,8,128]{3,2,1,0:T(8,128)} %fusion.30, s32[]{:T(128)} %constant.102.clone.1), window={size=1x1x1x128 pad=0_0x0_0x0_0x127_0}, to_apply=%region_0.1 | reduce-window | flops 33292288 | bytes 2097156 | tf_op jit(solution)/shard_map/reduce-window
  137.0 1.3 slice.138
  138.3 2.0 copy.13
  140.5 1.3 broadcast_add_fusion
  141.8 1.4 reduce_window_sum.31
  143.6 7.1 scatter_custom_fusion.1
  150.7 12.4 all-to-all-start
  163.5 36.3 %reduce-window.16 = s32[2,16,16,4,128]{4,2,3,1,0:T(8,128)S(1)} reduce-window(s32[2,16,16,4,128]{4,2,3,1,0:T(8,128)S(1)} %fusion.31, s32[]{:T(128)} %constant.102.clone.1), window={size=1x1x1x1x128 pad=0_0x0_0x0_0x0_0x127_0}, to_apply=%region_4.5 | reduce-window | flops 33292288 | bytes 2097156 | tf_op jit(solution)/shard_map/reduce-window.2
  201.9 59.7 %all-to-all-done = f32[16,128,512]{2,1,0:T(8,128)} async-done(((f32[16,128,512]{2,1,0:T(8,128)}), f32[16,128,512]{2,1,0:T(8,128)}, u32[]{:S(2)}, u32[]{:S(2)}) %all-to-all-start) | async-done | bytes 4194336 | tf_op jit(solution)/shard_map/all_to_all | solution.py:83
  261.6 4.2 fusion.95
  265.7 1.8 copy.27
  267.6 1.9 copy.28
  269.5 6.0 scatter_custom_fusion.2
  275.5 4.6 scatter_custom_fusion.3
  280.1 2.1 bitcast_dynamic-update-slice_fusion.14
  282.6 1.3 copy-done.3
  283.9 0.9 bitcast_dynamic-update-slice_fusion.13
  286.5 0.9 bitcast_dynamic-update-slice_fusion.10
  289.8 0.9 bitcast_dynamic-update-slice_fusion.6
  290.7 0.9 bitcast_dynamic-update-slice_fusion.5
  296.6 5.8 all-to-all-start.1
  303.2 60.3 %scatter_custom_fusion.8 = s32[2048]{0:T(1024)S(1)} fusion(s32[16384]{0:T(1024)S(1)} %bitcast.239, s32[16384]{0:T(1024)S(1)} %bitcast.240, s32[]{:T(128)} %constant.100.clone.1), kind=kCustom, calls=%fused_computation.210 | custom fusion | bytes 8196
  364.0 60.3 %scatter_custom_fusion = s32[2048]{0:T(1024)S(1)} fusion(s32[16384]{0:T(1024)S(1)} %bitcast.238, s32[16384]{0:T(1024)S(1)} %add_select_fusion.4, s32[]{:T(128)} %constant.100.clone.1), kind=kCustom, calls=%fused_computation.212 | custom fusion | bytes 8196 | tf_op jit(solution)/shard_map/scatter | solution.py:37
  424.4 64.2 %all-to-all-done.1 = f32[16,2,1024,64]{2,3,1,0:T(8,128)} async-done(((f32[16,2,1024,64]{2,3,1,0:T(8,128)}), f32[16,2,1024,64]{2,3,1,0:T(8,128)}, u32[]{:S(2)}, u32[]{:S(2)}) %all-to-all-start.1) | async-done | bytes 8388640 | tf_op jit(solution)/shard_map/all_to_all | solution.py:90
  488.5 8.4 fusion.94
  496.9 12.6 scatter_custom_fusion.6
  509.6 5.4 copy.21
  514.9 12.5 scatter_custom_fusion.4
  527.4 5.3 copy.20
  532.8 14.4 scatter_fusion
  547.2 14.4 scatter_fusion.1
  561.7 1.7 fusion.47
  564.5 174.2 %all-reduce.6.cloned.1.call-done = f32[384,128]{0,1:T(8,128)} async-done(((f32[384,128]{0,1:T(8,128)}), f32[384,128]{0,1:T(8,128)}) %all-reduce.6.cloned.1.call-update) | async-done | bytes 196624 | tf_op jit(solution)/shard_map/psum | solution.py:9
  738.7 2.1 convolution_subtract_fusion.2
  742.2 0.9 fusion.98
  743.1 184.5 %all-reduce.8.cloned.1.call-done = f32[256,128]{0,1:T(8,128)} async-done(((f32[256,128]{0,1:T(8,128)}), f32[256,128]{0,1:T(8,128)}) %all-reduce.8.cloned.1.call-update) | async-done | bytes 131088 | tf_op jit(solution)/shard_map/psum | solution.py:9
  927.6 0.9 fusion.99
  928.5 2.9 convolution_subtract_fusion.1
  932.8 178.0 %all-reduce.10.cloned.1.call-done = f32[128,128]{0,1:T(8,128)} async-done(((f32[128,128]{0,1:T(8,128)}), f32[128,128]{0,1:T(8,128)}) %all-reduce.10.cloned.1.call-update) | async-done | bytes 65552 | tf_op jit(solution)/shard_map/psum | solution.py:9
  1110.7 3.8 fusion.19
  1115.2 1.6 maximum_select_fusion
  1116.9 166.6 %all-reduce.12.cloned.1.call-done = f32[1024,512]{0,1:T(8,128)} async-done(((f32[1024,512]{0,1:T(8,128)}), f32[1024,512]{0,1:T(8,128)}) %all-reduce.12.cloned.1.call-update) | async-done | bytes 2097168 | tf_op jit(solution)/shard_map/psum | solution.py:9
  1283.4 4.1 fusion.96
  1287.5 1.3 copy.26
  1288.9 210.5 %all-reduce.14.cloned.1.call-done = f32[1024,512]{0,1:T(8,128)} async-done(((f32[1024,512]{0,1:T(8,128)}), f32[1024,512]{0,1:T(8,128)}) %all-reduce.14.cloned.1.call-update) | async-done | bytes 2097168 | tf_op jit(solution)/shard_map/psum | solution.py:9
  1499.3 10.8 convolution_subtract_fusion
  (87 shorter events, 18.4 us)
Async XLA Ops:
  7.2 136.5 %copy-start = (f32[1,1024,512]{2,1,0:T(8,128)S(1)}, f32[1,1024,512]{2,1,0:T(8,128)}, u32[]{:S(2)}) copy-start(f32[1,1024,512]{2,1,0:T(8,128)} %param.5) | copy-start | bytes 6291460
  7.2 5.0 copy-start.4
  150.7 110.8 %all-to-all-start = ((f32[16,128,512]{2,1,0:T(8,128)}), f32[16,128,512]{2,1,0:T(8,128)}, u32[]{:S(2)}, u32[]{:S(2)}) async-start(f32[16,128,512]{2,1,0:T(8,128)} %bitcast.223), calls=%async_computation | async-start | bytes 8388608 | tf_op jit(solution)/shard_map/all_to_all | solution.py:83
  280.1 2.5 copy-start.2
  280.1 3.8 copy-start.3
  296.6 6.0 copy-start.7
  296.6 6.1 copy-start.6
  296.6 6.5 copy-start.5
  296.6 191.9 %all-to-all-start.1 = ((f32[16,2,1024,64]{2,3,1,0:T(8,128)}), f32[16,2,1024,64]{2,3,1,0:T(8,128)}, u32[]{:S(2)}, u32[]{:S(2)}) async-start(f32[16,2,1024,64]{2,3,1,0:T(8,128)} %fusion.50), calls=%async_computation.1 | async-start | bytes 16777216 | tf_op jit(solution)/shard_map/all_to_all | solution.py:90
  302.4 436.3 %all-reduce.6.cloned.1.call-start = ((), (), s32[]{:S(2)}) async-start(), calls=%async_computation.2 | async-start | bytes 393216 | tf_op jit(solution)/shard_map/psum | solution.py:9
  564.1 363.5 %all-reduce.8.cloned.1.call-start = ((), (), s32[]{:S(2)}) async-start(), calls=%async_computation.3 | async-start | bytes 262144 | tf_op jit(solution)/shard_map/psum | solution.py:9
  742.1 368.6 %all-reduce.10.cloned.1.call-start = ((), (), s32[]{:S(2)}) async-start(), calls=%async_computation.4 | async-start | bytes 131072 | tf_op jit(solution)/shard_map/psum | solution.py:9
  932.6 350.8 %all-reduce.12.cloned.1.call-start = ((), (), s32[]{:S(2)}) async-start(), calls=%async_computation.5 | async-start | bytes 4194304 | tf_op jit(solution)/shard_map/psum | solution.py:9
  1116.8 382.5 %all-reduce.14.cloned.1.call-start = ((), (), s32[]{:S(2)}) async-start(), calls=%async_computation.6 | async-start | bytes 4194304 | tf_op jit(solution)/shard_map/psum | solution.py:9
  1287.5 222.6 %copy-start.1 = (f32[1,1024,512]{2,1,0:T(8,128)S(1)}, f32[1,1024,512]{2,1,0:T(8,128)}, u32[]{:S(2)}) copy-start(f32[1,1024,512]{2,1,0:T(8,128)} %param.5) | copy-start | bytes 6291460
Sparse Core Ops, SparseCore 0:
  564.2 174.5 all-reduce.5
  742.3 185.2 all-reduce.7
  932.7 177.9 all-reduce.9
  1116.9 166.4 all-reduce.11
  1287.6 211.6 all-reduce.13
